TPU v7x, 128 devices: a whole 4x4x4 slice. The times are simulated.
128 devices in a mesh: gx: 32 (over z, x, y_hi), gy: 4 (over y_lo, core).
Axes of the slice: x: 4, y: 4 (y_hi: 2, y_lo: 2; y = y_hi * 2 + y_lo), z: 4, core: 2. Of those that a mesh axis runs over, the one named last changes fastest.
Arguments:
- rhs_field: float32 [2, 8, 256, 1024], P(None, None, 'gx', 'gy'), may hold values from -6 to 6
- permittivity: float32 [8, 256, 1024], P(None, 'gx', 'gy'), may hold values from 1 to 4
- surf_dist: float32 [16384, 128], P(('gx', 'gy')), may hold values from 0.2 to 1
- surf_normal: float32 [3, 16384, 128], P(None, ('gx', 'gy')), may hold values from -4 to 4
- surf_inc: float32 [2, 16384, 128], P(None, ('gx', 'gy')), may hold values from -6 to 6
- surf_cell: int32 [16384, 128], P(('gx', 'gy')), may hold values from 0 to 16383
- surf_mask: int32 [16384, 128], P(('gx', 'gy')), may hold values 0 or 1
- surf_owner: int32 [16384, 1], P(('gx', 'gy')), may hold values from 0 to 127; in each aligned block of 128 rows (0 to 127, 128 to 255, ...) at most 2 rows name the same one
Outputs:
- solution: float32 [2, 8, 256, 1024], P(None, None, 'gx', 'gy')
- residual: float32 [2, 8, 256, 1024], P(None, None, 'gx', 'gy')
Inputs may be any that keep to these rules, and one draw needn't show every extreme that they name: `surf_owner`: within the 128 rows of one device no owner is named more than 2 times, a bound that some block reaches.
All inputs are finite; a program needn't handle non-finite values. No bound on the sum of `surf_mask` on one device may be relied on, other than what follows from the above.
Results may differ from a plain program's by a relative error of at most 0.00002.
Values sent between devices are 32-bit elements; how exact they have to be, the bound alone decides.
No kernel may reach another device: no remote copies, remote signals or barrier semaphores. Data moves between devices by JAX's collectives and lax.ppermute only.
A program may use at most 128 MiB of HBM per device.

v0:
```python
import jax
import jax.numpy as jnp
from jax import lax
from jax.sharding import PartitionSpec as P

CAP = 2
ITERS = 2


K_SQUARED = 0.25
BETA = 0.5
OMEGA = 0.8
TAU = 1.0


def with_halo(shard, sides, width):
    for axis, dim in sides:
        size, length = (lax.axis_size(axis), shard.shape[dim])
        up = [(i, (i + 1) % size) for i in range(size - 1)]
        down = [(j, i) for i, j in up]
        last = lax.slice_in_dim(shard, length - width, length, axis=dim)
        first = lax.slice_in_dim(shard, 0, width, axis=dim)
        before = lax.ppermute(last, axis, up)
        after = lax.ppermute(first, axis, down)
        shard = jnp.concatenate([before, shard, after], axis=dim)
    return shard


def padded_field(field):
    framed = with_halo(field, (("gx", 2), ("gy", 3)), 1)
    return jnp.pad(framed, ((0, 0), (1, 1), (0, 0), (0, 0)))


def apply_helm(padded, perm):
    center = padded[:, 1:-1, 1:-1, 1:-1]
    beside = padded[:, 2:, 1:-1, 1:-1] + padded[:, :-2, 1:-1, 1:-1]
    beside = beside + padded[:, 1:-1, 2:, 1:-1] + padded[:, 1:-1, :-2, 1:-1]
    beside = beside + padded[:, 1:-1, 1:-1, 2:] + padded[:, 1:-1, 1:-1, :-2]
    return (6.0 - K_SQUARED * perm)[None] * center - beside


def complex_divide(vec, inv_real, inv_imag):
    return jnp.stack([vec[0] * inv_real - vec[1] * inv_imag, vec[0] * inv_imag + vec[1] * inv_real])


def per_device(
    rhs_field, permittivity, surf_dist, surf_normal, surf_inc, surf_cell, surf_mask, surf_owner
):
    rows_dev = rhs_field.shape[2]
    cols_dev = rhs_field.shape[3]
    planes = rhs_field.shape[1]
    grid_x = lax.axis_size("gx")
    grid_y = lax.axis_size("gy")
    devices = grid_x * grid_y
    points = surf_cell.shape[1]
    owner_ids = surf_owner[:, 0]
    onehot = (owner_ids[:, None] == jnp.arange(devices, dtype=jnp.int32)[None, :]).astype(jnp.int32)
    slot_rank = jnp.sum((jnp.cumsum(onehot, axis=0) - onehot) * onehot, axis=1)
    slot_index = owner_ids * CAP + slot_rank
    float_data = jnp.concatenate([surf_dist[None], surf_normal, surf_inc], axis=0)
    int_data = jnp.stack([surf_cell, surf_mask])
    float_send = (
        jnp.zeros((6, devices * CAP, points), jnp.float32).at[:, slot_index, :].set(float_data)
    )
    int_send = jnp.zeros((2, devices * CAP, points), jnp.int32).at[:, slot_index, :].set(int_data)
    float_recv, int_recv = (
        lax.all_to_all(float_send, ("gx", "gy"), split_axis=1, concat_axis=1, tiled=True),
        lax.all_to_all(int_send, ("gx", "gy"), split_axis=1, concat_axis=1, tiled=True),
    )
    dist = float_recv[0].reshape(-1)
    normal = float_recv[1:4].reshape(3, -1)
    incident = float_recv[4:6].reshape(2, -1)
    cells = int_recv[0].reshape(-1)
    weight = TAU * int_recv[1].reshape(-1).astype(jnp.float32)
    per_plane = rows_dev * cols_dev
    diag_real = 6.0 - K_SQUARED * permittivity
    diag_imag = BETA * K_SQUARED * permittivity
    denom = diag_real * diag_real + diag_imag * diag_imag
    inv_real = diag_real / denom
    inv_imag = -diag_imag / denom
    solution = jnp.zeros_like(rhs_field)
    residual = rhs_field
    for outer_no in range(ITERS):
        padded = padded_field(solution)
        image = apply_helm(padded, permittivity)
        center = padded[:, 1:-1, 1:-1, 1:-1]
        diff_z = padded[:, 2:, 1:-1, 1:-1] - padded[:, :-2, 1:-1, 1:-1]
        diff_x = padded[:, 1:-1, 2:, 1:-1] - padded[:, 1:-1, :-2, 1:-1]
        diff_y = padded[:, 1:-1, 1:-1, 2:] - padded[:, 1:-1, 1:-1, :-2]
        features = jnp.stack([center, diff_z, diff_x, diff_y]).reshape(8, -1)
        picked = jnp.take(features, cells, axis=1).reshape(4, 2, -1)
        grad_dot = normal[0] * picked[1]
        grad_dot = grad_dot + normal[1] * picked[2]
        grad_dot = grad_dot + normal[2] * picked[3]
        penalty = weight * (picked[0] + dist * grad_dot * 0.5 + incident)
        surface = jnp.zeros((2, planes * per_plane), jnp.float32).at[:, cells].add(penalty)
        residual = rhs_field - image - surface.reshape(rhs_field.shape)
        update = OMEGA * complex_divide(residual, inv_real, inv_imag)
        image_z = apply_helm(padded_field(update), permittivity)
        shifted = jnp.stack(
            [image_z[0] - diag_imag * update[1], image_z[1] + diag_imag * update[0]]
        )
        update = update + OMEGA * complex_divide(residual - shifted, inv_real, inv_imag)
        solution = solution + update
    return (solution, residual)


def solution(mesh):
    placed = (
        P(None, None, "gx", "gy"),
        P(None, "gx", "gy"),
        P(("gx", "gy"), None),
        P(None, ("gx", "gy"), None),
        P(None, ("gx", "gy"), None),
        P(("gx", "gy"), None),
        P(("gx", "gy"), None),
        P(("gx", "gy"), None),
    )
    return jax.shard_map(
        per_device,
        mesh=mesh,
        in_specs=placed,
        out_specs=(P(None, None, "gx", "gy"), P(None, None, "gx", "gy")),
        check_vma=False,
    )
```

profile of v0, /device:TPU:1, one launch (start us, length us, event | category | flops | bytes accessed | tf_op | source)
XLA Modules:
  0.0 837.3 jit_solution(6516538168164613892)
XLA Ops:
  0.6 1.3 collective-permute-start.1
  1.9 6.3 collective-permute-start
  8.2 0.7 fusion.47
  9.1 0.8 select_reduce_fusion
  10.0 0.7 fusion.48
  10.6 0.9 add_bitcast_fusion
  11.6 0.8 broadcast_in_dim.36
  12.4 12.3 %scatter_fusion = s32[2,256,128]{2,0,1:T(2,128)} fusion(s32[2,256,128]{2,0,1:T(2,128)} %broadcast_in_dim.36, s32[128]{0:T(128)S(1)} %fusion.48, s32[128,2,128]{2,1,0:T(2,128)S(1)} %copy.24), kind=kCustom, calls=%fused_computation.2 | custom fusion | bytes 393728 | tf_op jit(solution)/shard_map/scatter | solution.py:65
  24.7 13.8 %all-to-all-start = ((s32[2,256,128]{2,0,1:T(2,128)}), s32[2,256,128]{2,0,1:T(2,128)S(1)}, u32[]{:S(2)}, u32[]{:S(2)}) async-start(s32[2,256,128]{2,0,1:T(2,128)} %scatter_fusion), calls=%async_computation | async-start | bytes 524288 | tf_op jit(solution)/shard_map/all_to_all | solution.py:68
  38.5 1.5 broadcast_multiply_fusion
  40.2 3.5 collective-permute-start.2
  43.8 1.9 collective-permute-start.3
  45.7 1.0 maximum_bitcast_fusion
  47.0 1.0 broadcast_in_dim.37
  48.0 12.3 %scatter_fusion.1 = f32[6,256,128]{2,0,1:T(8,128)} fusion(f32[6,256,128]{2,0,1:T(8,128)} %broadcast_in_dim.37, s32[128]{0:T(128)S(1)} %fusion.48, f32[128,6,128]{2,1,0:T(8,128)S(1)} %copy.27), kind=kCustom, calls=%fused_computation.3 | custom fusion | bytes 1180160 | tf_op jit(solution)/shard_map/scatter | solution.py:63
  60.4 0.3 select_maximum_fusion.12
  60.7 0.8 copy-done.1
  62.1 5.3 copy.25
  67.4 9.7 %all-to-all-start.1 = ((f32[6,256,128]{2,0,1:T(8,128)}), f32[6,256,128]{2,0,1:T(8,128)S(1)}, u32[]{:S(2)}, u32[]{:S(2)}) async-start(f32[6,256,128]{2,0,1:T(8,128)} %scatter_fusion.1), calls=%async_computation.1 | async-start | bytes 2097152 | tf_op jit(solution)/shard_map/all_to_all | solution.py:67
  77.0 0.8 slice_convert_fusion
  77.9 0.7 compare_and_fusion
  78.6 0.7 copy-done.3
  79.2 112.4 %gather_fusion = f32[32768,8]{1,0:T(8,128)} fusion(f32[8,16384]{0,1:T(8,128)} %copy.25, s32[32768]{0:T(1024)S(1)} %fusion.33), kind=kCustom, calls=%fused_computation.clone | custom fusion | bytes 2228224 | tf_op jit(solution)/shard_map/jit(_take)/gather | solution.py:91
  191.6 9.7 %copy.26 = f32[32768,8]{0,1:T(8,128)S(1)} copy(f32[32768,8]{1,0:T(8,128)} %gather_fusion) | data formatting | bytes 2097152 | tf_op jit(solution)/shard_map/jit(_take)/gather | solution.py:91
  201.3 0.9 select_bitcast_fusion.1
  202.4 0.4 fusion.49
  202.8 0.6 copy-done.11
  203.5 1.5 multiply_bitcast_fusion.1
  205.0 8.2 copy.28
  213.3 205.9 %scatter_custom_fusion.2 = f32[2,16384]{0,1:T(8,128)} fusion(s32[32768]{0:T(1024)S(1)} %bitcast.208, f32[32768,2]{1,0:T(8,128)} %copy.28, f32[]{:T(128)} %constant.20.clone.1), kind=kCustom, calls=%fused_computation.8 | custom fusion | flops 65536 | bytes 131584 | tf_op jit(solution)/shard_map/scatter-add | solution.py:96
  419.2 5.2 copy.29
  424.5 0.3 subtract_subtract_fusion.1
  424.9 4.8 collective-permute-start.4
  429.6 1.3 collective-permute-start.5
  431.0 4.7 collective-permute-done.5
  435.8 2.2 collective-permute-start.7
  438.0 4.3 collective-permute-start.6
  442.3 0.5 collective-permute-done.7
  442.9 1.2 collective-permute-done.6
  444.1 0.3 select_maximum_fusion.8
  444.8 0.7 multiply_subtract_fusion
  445.5 5.4 collective-permute-start.8
  450.9 1.3 collective-permute-start.9
  452.2 4.7 collective-permute-done.9
  457.0 5.2 collective-permute-start.10
  462.2 1.9 collective-permute-start.11
  464.2 4.3 collective-permute-done.11
  468.5 0.3 select_maximum_fusion.4
  469.3 5.3 copy.30
  474.5 112.4 %gather_fusion.1 = f32[32768,8]{1,0:T(8,128)} fusion(f32[8,16384]{0,1:T(8,128)} %copy.30, s32[32768]{0:T(1024)S(1)} %copy-done.4), kind=kCustom, calls=%fused_computation.1.clone | custom fusion | bytes 2228224 | tf_op jit(solution)/shard_map/jit(_take)/gather | solution.py:91
  586.9 9.7 %copy.31 = f32[32768,8]{0,1:T(8,128)S(1)} copy(f32[32768,8]{1,0:T(8,128)} %gather_fusion.1) | data formatting | bytes 2097152 | tf_op jit(solution)/shard_map/jit(_take)/gather | solution.py:91
  596.8 1.6 multiply_bitcast_fusion
  598.5 8.2 copy.32
  606.7 205.9 %scatter_custom_fusion.3 = f32[2,16384]{0,1:T(8,128)} fusion(s32[32768]{0:T(1024)} %bitcast.209, f32[32768,2]{1,0:T(8,128)} %copy.32, f32[]{:T(128)} %constant.20.clone.1), kind=kCustom, calls=%fused_computation.6 | custom fusion | flops 65536 | bytes 131584 | tf_op jit(solution)/shard_map/scatter-add | solution.py:96
  812.6 5.2 copy.33
  818.2 4.0 collective-permute-start.12
  822.2 1.3 collective-permute-start.13
  823.5 4.7 collective-permute-done.13
  828.3 1.9 collective-permute-start.15
  830.3 3.6 collective-permute-start.14
  833.9 0.7 collective-permute-done.15
  834.6 1.2 collective-permute-done.14
  835.8 0.3 select_maximum_fusion
  836.6 0.7 fusion.30
  (104 shorter events, 3.9 us)
Async XLA Ops:
  0.6 39.4 %collective-permute-start.1 = (f32[2,8,1,256]{3,2,1,0:T(1,128)S(1)}, f32[2,8,1,256]{3,2,1,0:T(1,128)S(1)}, u32[]{:S(2)}, u32[]{:S(2)}) collective-permute-start(f32[2,8,1,256]{3,2,1,0:T(1,128)S(1)} %broadcast.87), channel_id=1, source_target_pairs={{4,0},{8,4},{12,8},{16,12},{20,16},{24,20},{28,24},{32,28},{36,32}... | collective-permute-start | bytes 49160 | tf_op jit(solution)/shard_map/ppermute | solution.py:24
  1.9 38.1 %collective-permute-start = (f32[2,8,1,256]{3,2,1,0:T(1,128)S(1)}, f32[2,8,1,256]{3,2,1,0:T(1,128)S(1)}, u32[]{:S(2)}, u32[]{:S(2)}) collective-permute-start(f32[2,8,1,256]{3,2,1,0:T(1,128)S(1)} %broadcast.87), channel_id=1, source_target_pairs={{0,4},{4,8},{8,12},{12,16},{16,20},{20,24},{24,28},{28,32},{32,36}... | collective-permute-start | bytes 49160 | tf_op jit(solution)/shard_map/ppermute | solution.py:23
  24.7 42.6 %all-to-all-start = ((s32[2,256,128]{2,0,1:T(2,128)}), s32[2,256,128]{2,0,1:T(2,128)S(1)}, u32[]{:S(2)}, u32[]{:S(2)}) async-start(s32[2,256,128]{2,0,1:T(2,128)} %scatter_fusion), calls=%async_computation | async-start | bytes 524288 | tf_op jit(solution)/shard_map/all_to_all | solution.py:68
  40.1 27.3 %copy-start.23 = (f32[2,8,1,256]{3,2,1,0:T(1,128)}, f32[2,8,1,256]{3,2,1,0:T(1,128)S(1)}, u32[]{:S(2)}) copy-start(f32[2,8,1,256]{3,2,1,0:T(1,128)S(1)} %collective-permute-done) | copy-start | bytes 49156
  40.2 20.1 %collective-permute-start.2 = (f32[2,8,10,1]{3,2,1,0:T(8,128)S(1)}, f32[2,8,10,1]{3,2,1,0:T(8,128)S(1)}, u32[]{:S(2)}, u32[]{:S(2)}) collective-permute-start(f32[2,8,10,1]{3,2,1,0:T(8,128)S(1)} %get-tuple-element.19), channel_id=1, source_target_pairs={{0,1},{1,2},{2,3},{4,5},{5,6},{6,7},{8,9},{9,10},{10,11},{12,13},{... | collective-permute-start | bytes 1928 | tf_op jit(solution)/shard_map/ppermute | solution.py:23
  43.8 16.6 %collective-permute-start.3 = (f32[2,8,10,1]{3,2,1,0:T(8,128)S(1)}, f32[2,8,10,1]{3,2,1,0:T(8,128)S(1)}, u32[]{:S(2)}, u32[]{:S(2)}) collective-permute-start(f32[2,8,10,1]{3,2,1,0:T(8,128)S(1)} %get-tuple-element.20), channel_id=1, source_target_pairs={{1,0},{2,1},{3,2},{5,4},{6,5},{7,6},{9,8},{10,9},{11,10},{13,12},{... | collective-permute-start | bytes 1928 | tf_op jit(solution)/shard_map/ppermute | solution.py:24
  60.4 1.5 copy-start.7
  60.4 7.0 copy-start.9
  60.7 0.8 copy-start.1
  67.4 135.0 %all-to-all-start.1 = ((f32[6,256,128]{2,0,1:T(8,128)}), f32[6,256,128]{2,0,1:T(8,128)S(1)}, u32[]{:S(2)}, u32[]{:S(2)}) async-start(f32[6,256,128]{2,0,1:T(8,128)} %scatter_fusion.1), calls=%async_computation.1 | async-start | bytes 2097152 | tf_op jit(solution)/shard_map/all_to_all | solution.py:67
  78.6 0.7 copy-start.3
  202.3 10.9 %copy-start.27 = (s32[32768,1]{0,1:T(1,128)}, s32[32768,1]{0,1:T(1,128)S(1)}, u32[]{:S(2)}) copy-start(s32[32768,1]{0,1:T(1,128)S(1)} %compare_select_fusion) | copy-start | bytes 393220
  202.7 0.7 copy-start.11
  202.7 0.7 copy-start.12
  202.8 0.8 copy-start.13
  213.3 211.1 %copy-start.2 = (f32[2,10,10,258]{3,2,1,0:T(8,128)S(1)}, f32[2,10,10,258]{3,2,1,0:T(8,128)}, u32[]{:S(2)}) copy-start(f32[2,10,10,258]{3,2,1,0:T(8,128)} %copy-done.1) | copy-start | bytes 619204
  213.3 211.2 %copy-start.8 = (f32[2,8,10,1]{3,2,1,0:T(8,128)S(1)}, f32[2,8,10,1]{3,2,1,0:T(8,128)}, u32[]{:S(2)}) copy-start(f32[2,8,10,1]{3,2,1,0:T(8,128)} %copy-done.7) | copy-start | bytes 1924
  213.3 211.2 %copy-start.10 = (f32[2,8,10,1]{3,2,1,0:T(8,128)S(1)}, f32[2,8,10,1]{3,2,1,0:T(8,128)}, u32[]{:S(2)}) copy-start(f32[2,8,10,1]{3,2,1,0:T(8,128)} %copy-done.9) | copy-start | bytes 1924
  213.3 211.2 %copy-start.18 = (f32[2,8,8,256]{3,2,1,0:T(8,128)S(1)}, f32[2,8,8,256]{3,2,1,0:T(8,128)}, u32[]{:S(2)}) copy-start(f32[2,8,8,256]{3,2,1,0:T(8,128)} %param.10) | copy-start | bytes 393220
  213.3 211.2 %copy-start.24 = (f32[2,8,1,256]{3,2,1,0:T(1,128)S(1)}, f32[2,8,1,256]{3,2,1,0:T(1,128)}, u32[]{:S(2)}) copy-start(f32[2,8,1,256]{3,2,1,0:T(1,128)} %copy-done.23) | copy-start | bytes 49156
  213.3 211.2 %copy-start.25 = (f32[8,8,256]{2,1,0:T(8,128)S(1)}, f32[8,8,256]{2,1,0:T(8,128)}, u32[]{:S(2)}) copy-start(f32[8,8,256]{2,1,0:T(8,128)} %get-tuple-element.39) | copy-start | bytes 196612
  213.3 211.5 %copy-start = (f32[8,8,256]{2,1,0:T(8,128)S(1)}, f32[8,8,256]{2,1,0:T(8,128)}, u32[]{:S(2)}) copy-start(f32[8,8,256]{2,1,0:T(8,128)} %param.11) | copy-start | bytes 196612
  213.3 231.1 %copy-start.16 = (f32[8,8,256]{2,1,0:T(8,128)S(1)}, f32[8,8,256]{2,1,0:T(8,128)}, u32[]{:S(2)}) copy-start(f32[8,8,256]{2,1,0:T(8,128)} %get-tuple-element.38) | copy-start | bytes 196612
  424.9 6.1 collective-permute-start.4
  429.6 6.0 collective-permute-start.5
  435.8 7.1 collective-permute-start.7
  438.0 6.1 collective-permute-start.6
  444.4 30.1 %copy-start.4 = (s32[32768]{0:T(1024)S(1)}, s32[32768]{0:T(1024)}, u32[]{:S(2)}) copy-start(s32[32768]{0:T(1024)} %copy-done.3) | copy-start | bytes 393220
  445.4 18.8 %copy-start.14 = (f32[8,8,256]{2,1,0:T(8,128)}, f32[8,8,256]{2,1,0:T(8,128)S(1)}, u32[]{:S(2)}) copy-start(f32[8,8,256]{2,1,0:T(8,128)S(1)} %get-tuple-element.26) | copy-start | bytes 196612
  445.5 6.7 collective-permute-start.8
  450.9 6.0 collective-permute-start.9
  456.9 17.7 %copy-start.21 = (f32[2,8,1,256]{3,2,1,0:T(1,128)}, f32[2,8,1,256]{3,2,1,0:T(1,128)S(1)}, u32[]{:S(2)}) copy-start(f32[2,8,1,256]{3,2,1,0:T(1,128)S(1)} %collective-permute-done.9) | copy-start | bytes 49156
  457.0 7.1 collective-permute-start.10
  462.2 6.3 collective-permute-start.11
  586.9 9.7 %copy-start.20 = (pred[32768]{0:T(1024)(128)(4,1)S(1)}, pred[32768]{0:T(1024)(128)(4,1)}, u32[]{:S(2)}) copy-start(pred[32768]{0:T(1024)(128)(4,1)} %compare_and_fusion) | copy-start | bytes 98308
  586.9 9.9 %copy-start.6 = (f32[1,256,128]{2,0,1:T(1,128)S(1)}, f32[1,256,128]{2,0,1:T(1,128)}, u32[]{:S(2)}) copy-start(f32[1,256,128]{2,0,1:T(1,128)} %get-tuple-element.17) | copy-start | bytes 393220
  606.7 211.1 %copy-start.19 = (f32[2,8,8,256]{3,2,1,0:T(8,128)S(1)}, f32[2,8,8,256]{3,2,1,0:T(8,128)}, u32[]{:S(2)}) copy-start(f32[2,8,8,256]{3,2,1,0:T(8,128)} %param.10) | copy-start | bytes 393220
  606.7 211.1 %copy-start.22 = (f32[2,8,1,256]{3,2,1,0:T(1,128)S(1)}, f32[2,8,1,256]{3,2,1,0:T(1,128)}, u32[]{:S(2)}) copy-start(f32[2,8,1,256]{3,2,1,0:T(1,128)} %copy-done.21) | copy-start | bytes 49156
  606.7 211.1 %copy-start.26 = (f32[8,8,256]{2,1,0:T(8,128)S(1)}, f32[8,8,256]{2,1,0:T(8,128)}, u32[]{:S(2)}) copy-start(f32[8,8,256]{2,1,0:T(8,128)} %get-tuple-element.37) | copy-start | bytes 196612
  606.7 229.5 %copy-start.17 = (f32[8,8,256]{2,1,0:T(8,128)S(1)}, f32[8,8,256]{2,1,0:T(8,128)}, u32[]{:S(2)}) copy-start(f32[8,8,256]{2,1,0:T(8,128)} %get-tuple-element.38) | copy-start | bytes 196612
  812.6 24.0 %copy-start.15 = (f32[8,8,256]{2,1,0:T(8,128)S(1)}, f32[8,8,256]{2,1,0:T(8,128)}, u32[]{:S(2)}) copy-start(f32[8,8,256]{2,1,0:T(8,128)} %copy-done.14) | copy-start | bytes 196612
  818.1 19.2 %copy-start.5 = (f32[2,8,8,256]{3,2,1,0:T(8,128)}, f32[2,8,8,256]{3,2,1,0:T(8,128)S(1)}, u32[]{:S(2)}) copy-start(f32[2,8,8,256]{3,2,1,0:T(8,128)S(1)} %subtract_subtract_fusion) | copy-start | bytes 393220
  818.2 5.3 collective-permute-start.12
  822.2 6.0 collective-permute-start.13
  828.3 6.3 collective-permute-start.15
  830.3 5.6 collective-permute-start.14
where the time goes:
time: 843 us; the launch traced here: 837 us
  other arithmetic  428 us (51%)
  local copies, waits for them, and re-layouts  312 us (37%)
  starting transfers between devices  73.7 us (9%)
  waiting for transfers between devices  22 us (3%)
    scatter-add x2, other arithmetic, per_device(): jnp.zeros((2, planes * per_plane), jnp.float32).at[:, cells].add(penalty)  412 us
    gather x4, local copies, waits for them, and re-layouts, per_device(): picked = jnp.take(features, cells, axis=1).reshape(4, 2, -1)  244 us
    ppermute x8, starting transfers between devices, with_halo(): before = lax.ppermute(last, axis, up)  37.1 us
    ppermute x8, waiting for transfers between devices, with_halo(): after = lax.ppermute(first, axis, down)  19.6 us
  transfers between devices with their start and end apart: 18, of which 8 were waited for; matrix products, arithmetic and copies ran while one was open for 20% of the time, Pallas kernels for 0%

commit v1 on v0

v1 whole, which is shorter than its diff:
```python
import functools

import jax
import jax.numpy as jnp
from jax import lax
from jax.experimental import pallas as pl
from jax.experimental.pallas import tpu as pltpu
from jax.sharding import PartitionSpec as P

CAP = 2
K_SQUARED = 0.25
BETA = 0.5
OMEGA = 0.8
TAU = 1.0

CHANNELS = 6
PARTS = 11
GROUP = 8

f32 = jnp.float32
bf16 = jnp.bfloat16


def pack_kernel(owner_ref, dist_ref, normal_ref, inc_ref, cell_ref, mask_ref, out_ref, count_ref, coef_ref):
    blocks = dist_ref.shape[0]
    devices = out_ref.shape[0] // (CAP * CHANNELS)
    out_ref[...] = jnp.full(out_ref.shape, -1.0, f32)
    half = 0.5 * TAU * dist_ref[...]
    for k in range(3):
        coef_ref[k] = half * normal_ref[k]
    for k in range(2):
        coef_ref[3 + k] = TAU * inc_ref[k]
    cells = jnp.where(mask_ref[...] > 0, cell_ref[...], 1 << 14)
    coef_ref[5] = cells.astype(f32)

    def clear(i, carry):
        count_ref[i] = 0
        return carry

    lax.fori_loop(0, devices, clear, 0, unroll=8)

    def place(b, carry):
        owner = owner_ref[b]
        rank = count_ref[owner]
        count_ref[owner] = rank + 1
        base = (owner * CAP + rank) * CHANNELS
        for c in range(CHANNELS):
            out_ref[pl.ds(base + c, 1), :] = coef_ref[c, pl.ds(b, 1), :]
        return carry

    lax.fori_loop(0, blocks, place, 0, unroll=4)


def shift_rows(x, amount):
    return pltpu.roll(x, amount % x.shape[1], axis=1)


def scatter_kernel(recv_ref, rhs_ref, perm_ref, r1_ref, wn_ref, up_ref, down_ref, first_ref, second_ref, a_ref, b_ref, acc_ref):
    slots = recv_ref.shape[0] // CHANNELS
    planes = rhs_ref.shape[1]
    hi_n = planes * 8
    lo_n = rhs_ref.shape[3]
    data = recv_ref[...]
    row = lax.broadcasted_iota(jnp.int32, data.shape, 0)
    is_cell = lax.rem(row, CHANNELS) == CHANNELS - 1
    cell = data.astype(jnp.int32)
    lead = data.astype(bf16).astype(f32)
    first_ref[...] = jnp.where(is_cell, (cell >> 8).astype(f32), lead)
    second_ref[...] = jnp.where(is_cell, (cell & 255).astype(f32), data - lead)
    acc_ref[...] = jnp.zeros(acc_ref.shape, f32)
    hi_iota = lax.broadcasted_iota(jnp.int32, (hi_n, 128), 0).astype(f32).astype(bf16)
    lo_iota = lax.broadcasted_iota(jnp.int32, (lo_n, 128), 0).astype(f32).astype(bf16)
    one = jnp.ones((), bf16)
    zero = jnp.zeros((), bf16)

    def spread(ref, index, n):
        tile = jnp.broadcast_to(ref[pl.ds(index, 1), :], (16, 128)).astype(bf16)
        return jnp.concatenate([tile] * (n // 16), axis=0)

    def step(g, carry):
        for j in range(GROUP):
            base = (g * GROUP + j) * CHANNELS
            lanes = pl.ds(j * 128, 128)
            hot = hi_iota == spread(first_ref, base + 5, hi_n)
            for c in range(5):
                a_ref[pl.ds(2 * c * hi_n, hi_n), lanes] = jnp.where(hot, spread(first_ref, base + c, hi_n), zero)
                a_ref[pl.ds((2 * c + 1) * hi_n, hi_n), lanes] = jnp.where(hot, spread(second_ref, base + c, hi_n), zero)
            a_ref[pl.ds(10 * hi_n, hi_n), lanes] = jnp.where(hot, one, zero)
            b_ref[:, lanes] = jnp.where(lo_iota == spread(second_ref, base + 5, lo_n), one, zero)
        acc_ref[...] += lax.dot_general(
            a_ref[...], b_ref[...], (((1,), (1,)), ((), ())), preferred_element_type=f32
        )
        return carry

    lax.fori_loop(0, slots // GROUP, step, 0)

    def channel(c):
        if c == 5:
            total = acc_ref[pl.ds(10 * hi_n, hi_n), :]
        else:
            total = acc_ref[pl.ds(2 * c * hi_n, hi_n), :] + acc_ref[pl.ds((2 * c + 1) * hi_n, hi_n), :]
        return total.reshape(planes, 8, lo_n)

    re = rhs_ref[0] - channel(3)
    im = rhs_ref[1] - channel(4)
    wn = [TAU * channel(5), channel(0), channel(1), channel(2)]
    r1_ref[0] = re
    r1_ref[1] = im
    for k in range(4):
        wn_ref[k] = wn[k]
    perm = perm_ref[...]
    sub = lax.broadcasted_iota(jnp.int32, (planes, 8, lo_n), 1)
    t = jnp.where(sub < 3, re, shift_rows(im, 3))
    t = jnp.where(sub < 6, t, jnp.where(sub == 6, shift_rows(wn[0], 6), shift_rows(wn[1], 7)))
    up_ref[:, 0:8, :] = t
    t = jnp.where(sub < 3, perm, jnp.where(sub == 3, shift_rows(wn[2], 3), shift_rows(wn[3], 4)))
    up_ref[:, 8:16, :] = t
    t = jnp.where(sub >= 5, re, shift_rows(im, -3))
    t = jnp.where(sub >= 2, t, jnp.where(sub == 1, shift_rows(wn[0], -6), shift_rows(wn[1], -7)))
    down_ref[:, 0:8, :] = t
    t = jnp.where(sub >= 5, perm, jnp.where(sub == 4, shift_rows(wn[2], -3), shift_rows(wn[3], -4)))
    down_ref[:, 8:16, :] = t


ROW_PLACE = ((0, 0, 3), (0, 3, 3), (1, 0, 3), (0, 6, 1), (0, 7, 1), (1, 3, 1), (1, 4, 1))
COL_PLACE = ((0, 3), (3, 3), (6, 3), (9, 1), (10, 1), (11, 1), (12, 1))


def halo_rows(c, above_ref, below_ref, lanes):
    tile, offset, width = ROW_PLACE[c]
    rows = pl.ds(tile * 8, 8)
    below = shift_rows(below_ref[:, rows, lanes], -offset)
    above = shift_rows(above_ref[:, rows, lanes], offset)
    sub = lax.broadcasted_iota(jnp.int32, below.shape, 1)
    return jnp.where(sub < width, below, jnp.where(sub >= 8 - width, above, 0.0))


def own_channel(c, r1_ref, perm_ref, wn_ref, lanes):
    if c < 2:
        return r1_ref[c, :, :, lanes]
    if c == 2:
        return perm_ref[:, :, lanes]
    return wn_ref[c - 3, :, :, lanes]


def strip_kernel(r1_ref, perm_ref, wn_ref, above_ref, below_ref, left_ref, right_ref):
    lo_n = perm_ref.shape[2]
    planes = perm_ref.shape[0]
    lane = lax.broadcasted_iota(jnp.int32, (planes, 16, 128), 2)
    for out_ref, start, sign in ((left_ref, 0, 1), (right_ref, lo_n - 128, -1)):
        lanes = pl.ds(start, 128)
        place = lane if sign > 0 else 127 - lane
        strip = jnp.zeros((planes, 16, 128), f32)
        for c in range(7):
            full = jnp.concatenate(
                [own_channel(c, r1_ref, perm_ref, wn_ref, lanes), halo_rows(c, above_ref, below_ref, lanes)], axis=1
            )
            offset, width = COL_PLACE[c]
            moved = pltpu.roll(full, (sign * offset) % 128, axis=2)
            strip = jnp.where((place >= offset) & (place < offset + width), moved, strip)
        out_ref[...] = strip


def final_kernel(r1_ref, perm_ref, wn_ref, above_ref, below_ref, fleft_ref, fright_ref, sol_ref, res_ref):
    lo_n = perm_ref.shape[2]
    planes = perm_ref.shape[0]
    wide = lo_n + 128
    lane = lax.broadcasted_iota(jnp.int32, (planes, 16, 128), 2)
    everything = pl.ds(0, lo_n)

    def extended(c):
        body = jnp.concatenate(
            [own_channel(c, r1_ref, perm_ref, wn_ref, everything), halo_rows(c, above_ref, below_ref, everything)], axis=1
        )
        offset, width = COL_PLACE[c]
        right = pltpu.roll(fright_ref[...], (-offset) % 128, axis=2)
        left = pltpu.roll(fleft_ref[...], offset, axis=2)
        side = jnp.where(lane < width, right, jnp.where(lane >= 128 - width, left, 0.0))
        return jnp.concatenate([body, side], axis=2)

    re, im, perm, w, nz, nx, ny = [extended(c) for c in range(7)]
    diag = 6.0 - K_SQUARED * perm
    shift = BETA * K_SQUARED * perm
    denom = diag * diag + shift * shift
    inside = perm > 0.5
    inv_re = jnp.where(inside, OMEGA * diag / denom, 0.0)
    inv_im = jnp.where(inside, -OMEGA * shift / denom, 0.0)

    def damp(a, b):
        return a * inv_re - b * inv_im, a * inv_im + b * inv_re

    def sides(v):
        nothing = jnp.zeros((1,) + v.shape[1:], f32)
        after = jnp.concatenate([v[1:], nothing], axis=0)
        before = jnp.concatenate([nothing, v[:-1]], axis=0)
        return (
            (after, before),
            (pltpu.roll(v, 15, axis=1), pltpu.roll(v, 1, axis=1)),
            (pltpu.roll(v, wide - 1, axis=2), pltpu.roll(v, 1, axis=2)),
        )

    def helm(v, pairs):
        total = pairs[0][0] + pairs[0][1]
        for a, b in pairs[1:]:
            total = total + a + b
        return diag * v - total

    def swept(a, b):
        za, zb = damp(a, b)
        ma = helm(za, sides(za)) - shift * zb
        mb = helm(zb, sides(zb)) + shift * za
        da, db = damp(a - ma, b - mb)
        return za + da, zb + db

    def surface(v, pairs):
        (a, b), (c, d), (e, f) = pairs
        return w * v + nz * (a - b) + nx * (c - d) + ny * (e - f)

    def remaining(r, v):
        pairs = sides(v)
        return r - helm(v, pairs) - surface(v, pairs)

    sa, sb = swept(re, im)
    ra, rb = remaining(re, sa), remaining(im, sb)
    ua, ub = swept(ra, rb)
    res_ref[0] = ra[:, 0:8, 0:lo_n]
    res_ref[1] = rb[:, 0:8, 0:lo_n]
    sol_ref[0] = (sa + ua)[:, 0:8, 0:lo_n]
    sol_ref[1] = (sb + ub)[:, 0:8, 0:lo_n]


def in_vmem(n):
    return [pl.BlockSpec(memory_space=pltpu.VMEM)] * n


def shape(*dims):
    return jax.ShapeDtypeStruct(dims, f32)


def per_device(rhs_field, permittivity, surf_dist, surf_normal, surf_inc, surf_cell, surf_mask, surf_owner):
    planes, rows, cols = permittivity.shape
    blocks, points = surf_cell.shape
    gx, gy = lax.axis_size("gx"), lax.axis_size("gy")
    devices = gx * gy
    slots = devices * CAP
    params = pltpu.CompilerParams(vmem_limit_bytes=48 << 20)
    send = pl.pallas_call(
        pack_kernel,
        out_shape=shape(slots * CHANNELS, points),
        in_specs=[pl.BlockSpec(memory_space=pltpu.SMEM)] + in_vmem(5),
        out_specs=pl.BlockSpec(memory_space=pltpu.VMEM),
        scratch_shapes=[pltpu.SMEM((devices,), jnp.int32), pltpu.VMEM((CHANNELS, blocks, points), f32)],
        compiler_params=params,
        name="pack",
    )(surf_owner[:, 0], surf_dist, surf_normal, surf_inc, surf_cell, surf_mask)
    recv = lax.all_to_all(send.reshape(-1), ("gx", "gy"), split_axis=0, concat_axis=0, tiled=True)
    recv = recv.reshape(slots * CHANNELS, points)
    field = shape(2, planes, rows, cols)
    r1, wn, up, down = pl.pallas_call(
        scatter_kernel,
        out_shape=(field, shape(4, planes, rows, cols), shape(planes, 16, cols), shape(planes, 16, cols)),
        in_specs=in_vmem(3),
        out_specs=tuple(in_vmem(4)),
        scratch_shapes=[
            pltpu.VMEM((slots * CHANNELS, points), f32),
            pltpu.VMEM((slots * CHANNELS, points), f32),
            pltpu.VMEM((PARTS * planes * rows, GROUP * points), bf16),
            pltpu.VMEM((cols, GROUP * points), bf16),
            pltpu.VMEM((PARTS * planes * rows, cols), f32),
        ],
        compiler_params=params,
        name="scatter",
    )(recv, rhs_field, permittivity)
    later = [(i, i + 1) for i in range(gx - 1)]
    above = lax.ppermute(down, "gx", later)
    below = lax.ppermute(up, "gx", [(j, i) for i, j in later])
    strip = shape(planes, 16, 128)
    to_left, to_right = pl.pallas_call(
        strip_kernel,
        out_shape=(strip, strip),
        in_specs=in_vmem(5),
        out_specs=tuple(in_vmem(2)),
        compiler_params=params,
        name="strips",
    )(r1, permittivity, wn, above, below)
    later = [(i, i + 1) for i in range(gy - 1)]
    from_left = lax.ppermute(to_right, "gy", later)
    from_right = lax.ppermute(to_left, "gy", [(j, i) for i, j in later])
    return pl.pallas_call(
        final_kernel,
        out_shape=(field, field),
        in_specs=in_vmem(7),
        out_specs=tuple(in_vmem(2)),
        compiler_params=params,
        name="final",
    )(r1, permittivity, wn, above, below, from_left, from_right)


def solution(mesh):
    split = ("gx", "gy")
    placed = (
        P(None, None, "gx", "gy"),
        P(None, "gx", "gy"),
        P(split, None),
        P(None, split, None),
        P(None, split, None),
        P(split, None),
        P(split, None),
        P(split, None),
    )
    return jax.shard_map(
        per_device,
        mesh=mesh,
        in_specs=placed,
        out_specs=(P(None, None, "gx", "gy"), P(None, None, "gx", "gy")),
        check_vma=False,
    )
```

time: 843 us -> 79.2 us (0.09)
  other arithmetic: 428 us -> 0 us
  local copies, waits for them, and re-layouts: 312 us -> 5.01 us
  starting transfers between devices: 73.7 us -> 8.33 us
  blocking collectives: 0 us -> 27.4 us
  Pallas kernels: 0 us -> 24.4 us
  waiting for transfers between devices: 22 us -> 13 us
    scatter-add x2 -> x0, other arithmetic: 412 us -> none  [per_device(): jnp.zeros((2, planes * per_plane), jnp.float32).at[:, cells].add(penalty)]
    gather x4 -> x0, local copies, waits for them, and re-layouts: 244 us -> none  [per_device(): picked = jnp.take(features, cells, axis=1).reshape(4, 2, -1)]
    ppermute x16 -> x4, starting transfers between devices: 50.3 us -> 8.33 us  [the longest x1 2.71 us: per_device(): above = lax.ppermute(down, 'gx', later)]
    all_to_all x0 -> x1, blocking collectives: none -> 27.4 us  [per_device(): lax.all_to_all(send.reshape(-1), ('gx', 'gy'), split_axis=0, concat_axis=...]
    scatter x2 -> x0, local copies, waits for them, and re-layouts: 24.6 us -> none  [the longest x1 12.3 us: per_device(): jnp.zeros((6, devices * CAP, points), jnp.float32).at[:, slot_index, :]]
    pallas_call x0 -> x4, Pallas kernels: none -> 24.4 us  [the longest x1 20.7 us: per_device(): pl.pallas_call(scatter_kernel, out_shape=(field, shape(4, planes, rows, c...]
    all_to_all x2 -> x0, starting transfers between devices: 23.5 us -> none  [the longest x1 13.8 us: per_device(): lax.all_to_all(int_send, ('gx', 'gy'), split_axis=1, concat_axis=1, tiled...]
    reshape x6 -> x0, local copies, waits for them, and re-layouts: 21.2 us -> none  [the longest x4 10.7 us: per_device(): features = jnp.stack([center, diff_z, diff_x, diff_y]).reshape(8, -1)]
  transfers between devices with their start and end apart: 18 -> 4, of which waited for: 8 -> 3; matrix products, arithmetic and copies ran while one was open for 20% -> 0% of each run, Pallas kernels for 0% -> 0%
where the time goes in v1:
time: 79.2 us; the launch traced here: 78.8 us
  blocking collectives  27.4 us (35%)
  Pallas kernels  24.4 us (31%)
  waiting for transfers between devices  13 us (16%)
  starting transfers between devices  8.33 us (11%)
  local copies, waits for them, and re-layouts  5.01 us (6%)
    all_to_all x1, blocking collectives, per_device(): lax.all_to_all(send.reshape(-1), ('gx', 'gy'), split_axis=0, concat_axis=...  27.4 us
    pallas_call x1, Pallas kernels, per_device(): pl.pallas_call(scatter_kernel, out_shape=(field, shape(4, planes, rows, c...  20.7 us
    ppermute x1, waiting for transfers between devices, per_device(): below = lax.ppermute(up, 'gx', [(j, i) for i, j in later])  9.17 us
    unnamed x16, local copies, waits for them, and re-layouts  5.01 us
    ppermute x1, waiting for transfers between devices, per_device(): from_right = lax.ppermute(to_left, 'gy', [(j, i) for i, j in later])  3.16 us
    ppermute x1, starting transfers between devices, per_device(): above = lax.ppermute(down, 'gx', later)  2.71 us
    ppermute x1, starting transfers between devices, per_device(): from_right = lax.ppermute(to_left, 'gy', [(j, i) for i, j in later])  2.41 us
    ppermute x1, starting transfers between devices, per_device(): from_left = lax.ppermute(to_right, 'gy', later)  1.92 us
  transfers between devices with their start and end apart: 4, of which 3 were waited for; matrix products, arithmetic and copies ran while one was open for 0% of the time, Pallas kernels for 0%

profile of v1, /device:TPU:1, one launch (start us, length us, event | category | flops | bytes accessed | tf_op | source)
XLA Modules:
  0.0 78.8 jit_solution(1610827319887139932)
XLA Ops:
  0.6 0.0 copy-start.7
  0.6 0.6 copy-done.7
  1.3 0.0 copy-start.1
  1.3 0.9 %copy-done.1 = f32[3,128,128]{2,1,0:T(8,128)S(1)} copy-done((f32[3,128,128]{2,1,0:T(8,128)S(1)}, f32[3,128,128]{2,1,0:T(8,128)}, u32[]{:S(2)}) %copy-start.1) | copy-done | bytes 196632
  2.2 0.0 copy-start.2
  2.2 0.9 %copy-done.2 = f32[2,128,128]{2,1,0:T(8,128)S(1)} copy-done((f32[2,128,128]{2,1,0:T(8,128)S(1)}, f32[2,128,128]{2,1,0:T(8,128)}, u32[]{:S(2)}) %copy-start.2) | copy-done | bytes 131096
  3.1 0.0 copy-start.4
  3.1 0.8 %copy-done.4 = f32[128,128]{1,0:T(8,128)S(1)} copy-done((f32[128,128]{1,0:T(8,128)S(1)}, f32[128,128]{1,0:T(8,128)}, u32[]{:S(2)}) %copy-start.4) | copy-done | bytes 65560
  4.0 0.0 copy-start.5
  4.0 0.8 %copy-done.5 = s32[128,128]{1,0:T(8,128)S(1)} copy-done((s32[128,128]{1,0:T(8,128)S(1)}, s32[128,128]{1,0:T(8,128)}, u32[]{:S(2)}) %copy-start.5) | copy-done | bytes 65560
  4.8 0.0 copy-start.6
  4.8 0.8 %copy-done.6 = s32[128,128]{1,0:T(8,128)S(1)} copy-done((s32[128,128]{1,0:T(8,128)S(1)}, s32[128,128]{1,0:T(8,128)}, u32[]{:S(2)}) %copy-start.6) | copy-done | bytes 65560
  5.6 1.5 %pack.1 = f32[1536,128]{1,0:T(8,128)S(1)} custom-call(s32[128]{0:T(128)S(1)} %bitcast.5, f32[128,128]{1,0:T(8,128)S(1)} %copy-done.4, f32[3,128,128]{2,1,0:T(8,128)S(1)} %copy-done.1, f32[2,128,128]{2,1,0:T(8,128)S(1)} %copy-done.2, s32[128,128]{1,0:T(8,128)S(1)} %copy-done.5, s32[128,128]{1,0:T(8,128)S(1)} %copy-done.6), custom_call_target="tpu_custom_call" | custom-call | tf_op jit(solution)/shard_map/pack/pallas_call | solution.py:247
  7.2 0.0 copy-start
  7.2 0.0 copy-start.3
  7.2 27.4 %all_to_all.9 = f32[128,1536,1]{1,2,0:T(1,128)S(1)} all-to-all(f32[128,1536,1]{1,2,0:T(1,128)S(1)} %bitcast.3), channel_id=1, replica_groups=mesh['gx'=32,'gy'=4] {'gx','gy'}, dimensions={0} | all-to-all | bytes 1572864 | tf_op jit(solution)/shard_map/all_to_all | solution.py:256
  34.7 0.0 copy-done
  34.7 0.0 copy-done.3
  34.7 20.7 %scatter.1 = (f32[2,8,8,256]{3,2,1,0:T(8,128)S(1)}, f32[4,8,8,256]{3,2,1,0:T(8,128)S(1)}, f32[8,16,256]{2,1,0:T(8,128)S(1)}, f32[8,16,256]{2,1,0:T(8,128)S(1)}) custom-call(f32[1536,128]{1,0:T(8,128)S(1)} %bitcast.4, f32[2,8,8,256]{3,2,1,0:T(8,128)S(1)} %copy-done.3, f32[8,8,256]{2,1,0:T(8,128)S(1)} %copy-done), custom_call_target="tpu_custom_call" | custom-call | tf_op jit(solution)/shard_map/scatter/pallas_call | solution.py:259
  55.4 2.7 %collective-permute-start = (f32[8,16,256]{2,1,0:T(8,128)S(1)}, f32[8,16,256]{2,1,0:T(8,128)S(1)}, u32[]{:S(2)}, u32[]{:S(2)}) collective-permute-start(f32[8,16,256]{2,1,0:T(8,128)S(1)} %get-tuple-element.10), channel_id=1, source_target_pairs={{0,4},{4,8},{8,12},{12,16},{16,20},{20,24},{24,28},{28,32},{32,36}... | collective-permute-start | bytes 393224 | tf_op jit(solution)/shard_map/ppermute | solution.py:275
  58.1 1.3 %collective-permute-start.1 = (f32[8,16,256]{2,1,0:T(8,128)S(1)}, f32[8,16,256]{2,1,0:T(8,128)S(1)}, u32[]{:S(2)}, u32[]{:S(2)}) collective-permute-start(f32[8,16,256]{2,1,0:T(8,128)S(1)} %get-tuple-element.11), channel_id=1, source_target_pairs={{4,0},{8,4},{12,8},{16,12},{20,16},{24,20},{28,24},{32,28},{36,32}... | collective-permute-start | bytes 393224 | tf_op jit(solution)/shard_map/ppermute | solution.py:276
  59.4 0.6 collective-permute-done.above_ref
  60.0 9.2 %collective-permute-done.1.below_ref = f32[8,16,256]{2,1,0:T(8,128)S(1)} collective-permute-done((f32[8,16,256]{2,1,0:T(8,128)S(1)}, f32[8,16,256]{2,1,0:T(8,128)S(1)}, u32[]{:S(2)}, u32[]{:S(2)}) %collective-permute-start.1) | collective-permute-done | bytes 131104 | tf_op jit(solution)/shard_map/ppermute | solution.py:276
  69.2 0.3 strips.1
  69.5 1.9 %collective-permute-start.2 = (f32[8,16,128]{2,1,0:T(8,128)S(1)}, f32[8,16,128]{2,1,0:T(8,128)S(1)}, u32[]{:S(2)}, u32[]{:S(2)}) collective-permute-start(f32[8,16,128]{2,1,0:T(8,128)S(1)} %get-tuple-element.12), channel_id=1, source_target_pairs={{0,1},{1,2},{2,3},{4,5},{5,6},{6,7},{8,9},{9,10},{10,11},{12,13},{... | collective-permute-start | bytes 196616 | tf_op jit(solution)/shard_map/ppermute | solution.py:287
  71.4 2.4 %collective-permute-start.3 = (f32[8,16,128]{2,1,0:T(8,128)S(1)}, f32[8,16,128]{2,1,0:T(8,128)S(1)}, u32[]{:S(2)}, u32[]{:S(2)}) collective-permute-start(f32[8,16,128]{2,1,0:T(8,128)S(1)} %get-tuple-element.13), channel_id=1, source_target_pairs={{1,0},{2,1},{3,2},{5,4},{6,5},{7,6},{9,8},{10,9},{11,10},{13,12},{... | collective-permute-start | bytes 196616 | tf_op jit(solution)/shard_map/ppermute | solution.py:288
  73.8 0.0 collective-permute-done.2.fleft_ref
  73.8 3.2 %collective-permute-done.3.fright_ref = f32[8,16,128]{2,1,0:T(8,128)S(1)} collective-permute-done((f32[8,16,128]{2,1,0:T(8,128)S(1)}, f32[8,16,128]{2,1,0:T(8,128)S(1)}, u32[]{:S(2)}, u32[]{:S(2)}) %collective-permute-start.3) | collective-permute-done | bytes 65568 | tf_op jit(solution)/shard_map/ppermute | solution.py:288
  77.0 1.8 %final.1 = (f32[2,8,8,256]{3,2,1,0:T(8,128)}, f32[2,8,8,256]{3,2,1,0:T(8,128)}) custom-call(f32[2,8,8,256]{3,2,1,0:T(8,128)S(1)} %get-tuple-element.8.r1_ref, f32[8,8,256]{2,1,0:T(8,128)S(1)} %copy-done, f32[4,8,8,256]{3,2,1,0:T(8,128)S(1)} %get-tuple-element.9.wn_ref, f32[8,16,256]{2,1,0:T(8,128)S(1)} %collective-permute-done.above_ref, ...), custom_call_target="tpu_custom_call" | custom-call | tf_op jit(solution)/shard_map/final/pallas_call | solution.py:289
Async XLA Ops:
  0.6 0.7 copy-start.7
  1.3 0.9 %copy-start.1 = (f32[3,128,128]{2,1,0:T(8,128)S(1)}, f32[3,128,128]{2,1,0:T(8,128)}, u32[]{:S(2)}) copy-start(f32[3,128,128]{2,1,0:T(8,128)} %normal_ref.1) | copy-start | bytes 589828
  2.2 0.9 %copy-start.2 = (f32[2,128,128]{2,1,0:T(8,128)S(1)}, f32[2,128,128]{2,1,0:T(8,128)}, u32[]{:S(2)}) copy-start(f32[2,128,128]{2,1,0:T(8,128)} %inc_ref.1) | copy-start | bytes 393220
  3.1 0.8 %copy-start.4 = (f32[128,128]{1,0:T(8,128)S(1)}, f32[128,128]{1,0:T(8,128)}, u32[]{:S(2)}) copy-start(f32[128,128]{1,0:T(8,128)} %dist_ref.1) | copy-start | bytes 196612
  4.0 0.8 %copy-start.5 = (s32[128,128]{1,0:T(8,128)S(1)}, s32[128,128]{1,0:T(8,128)}, u32[]{:S(2)}) copy-start(s32[128,128]{1,0:T(8,128)} %cell_ref.1) | copy-start | bytes 196612
  4.8 0.8 %copy-start.6 = (s32[128,128]{1,0:T(8,128)S(1)}, s32[128,128]{1,0:T(8,128)}, u32[]{:S(2)}) copy-start(s32[128,128]{1,0:T(8,128)} %mask_ref.1) | copy-start | bytes 196612
  7.2 27.5 %copy-start = (f32[8,8,256]{2,1,0:T(8,128)S(1)}, f32[8,8,256]{2,1,0:T(8,128)}, u32[]{:S(2)}) copy-start(f32[8,8,256]{2,1,0:T(8,128)} %perm_ref.5) | copy-start | bytes 196612
  7.2 27.5 %copy-start.3 = (f32[2,8,8,256]{3,2,1,0:T(8,128)S(1)}, f32[2,8,8,256]{3,2,1,0:T(8,128)}, u32[]{:S(2)}) copy-start(f32[2,8,8,256]{3,2,1,0:T(8,128)} %rhs_ref.1) | copy-start | bytes 393220
  55.4 4.6 %collective-permute-start = (f32[8,16,256]{2,1,0:T(8,128)S(1)}, f32[8,16,256]{2,1,0:T(8,128)S(1)}, u32[]{:S(2)}, u32[]{:S(2)}) collective-permute-start(f32[8,16,256]{2,1,0:T(8,128)S(1)} %get-tuple-element.10), channel_id=1, source_target_pairs={{0,4},{4,8},{8,12},{12,16},{16,20},{20,24},{24,28},{28,32},{32,36}... | collective-permute-start | bytes 393224 | tf_op jit(solution)/shard_map/ppermute | solution.py:275
  58.1 11.1 %collective-permute-start.1 = (f32[8,16,256]{2,1,0:T(8,128)S(1)}, f32[8,16,256]{2,1,0:T(8,128)S(1)}, u32[]{:S(2)}, u32[]{:S(2)}) collective-permute-start(f32[8,16,256]{2,1,0:T(8,128)S(1)} %get-tuple-element.11), channel_id=1, source_target_pairs={{4,0},{8,4},{12,8},{16,12},{20,16},{24,20},{28,24},{32,28},{36,32}... | collective-permute-start | bytes 393224 | tf_op jit(solution)/shard_map/ppermute | solution.py:276
  69.5 4.3 %collective-permute-start.2 = (f32[8,16,128]{2,1,0:T(8,128)S(1)}, f32[8,16,128]{2,1,0:T(8,128)S(1)}, u32[]{:S(2)}, u32[]{:S(2)}) collective-permute-start(f32[8,16,128]{2,1,0:T(8,128)S(1)} %get-tuple-element.12), channel_id=1, source_target_pairs={{0,1},{1,2},{2,3},{4,5},{5,6},{6,7},{8,9},{9,10},{10,11},{12,13},{... | collective-permute-start | bytes 196616 | tf_op jit(solution)/shard_map/ppermute | solution.py:287
  71.4 5.6 %collective-permute-start.3 = (f32[8,16,128]{2,1,0:T(8,128)S(1)}, f32[8,16,128]{2,1,0:T(8,128)S(1)}, u32[]{:S(2)}, u32[]{:S(2)}) collective-permute-start(f32[8,16,128]{2,1,0:T(8,128)S(1)} %get-tuple-element.13), channel_id=1, source_target_pairs={{1,0},{2,1},{3,2},{5,4},{6,5},{7,6},{9,8},{10,9},{11,10},{13,12},{... | collective-permute-start | bytes 196616 | tf_op jit(solution)/shard_map/ppermute | solution.py:288

commit v2 on v1

--- a/solution.py
+++ b/solution.py
@@ -15,59 +15,94 @@
 
 CHANNELS = 6
 PARTS = 11
-GROUP = 8
+GROUP = 32
 
 f32 = jnp.float32
 bf16 = jnp.bfloat16
 
 
-def pack_kernel(owner_ref, dist_ref, normal_ref, inc_ref, cell_ref, mask_ref, out_ref, count_ref, coef_ref):
+def pack_kernel(
+    owner_hbm, dist_hbm, normal_hbm, inc_hbm, cell_hbm, mask_hbm, out_ref,
+    owner_ref, base_ref, count_ref, dist_ref, coef_ref, cell_ref, mask_ref, sems,
+):
     blocks = dist_ref.shape[0]
-    devices = out_ref.shape[0] // (CAP * CHANNELS)
+    devices = count_ref.shape[0]
+    copies = [
+        pltpu.make_async_copy(owner_hbm, owner_ref, sems.at[0]),
+        pltpu.make_async_copy(dist_hbm, dist_ref, sems.at[1]),
+        pltpu.make_async_copy(normal_hbm, coef_ref.at[pl.ds(0, 3)], sems.at[2]),
+        pltpu.make_async_copy(inc_hbm, coef_ref.at[pl.ds(3, 2)], sems.at[3]),
+        pltpu.make_async_copy(cell_hbm, cell_ref, sems.at[4]),
+        pltpu.make_async_copy(mask_hbm, mask_ref, sems.at[5]),
+    ]
+    for copy in copies:
+        copy.start()
     out_ref[...] = jnp.full(out_ref.shape, -1.0, f32)
-    half = 0.5 * TAU * dist_ref[...]
-    for k in range(3):
-        coef_ref[k] = half * normal_ref[k]
-    for k in range(2):
-        coef_ref[3 + k] = TAU * inc_ref[k]
-    cells = jnp.where(mask_ref[...] > 0, cell_ref[...], 1 << 14)
-    coef_ref[5] = cells.astype(f32)
 
     def clear(i, carry):
         count_ref[i] = 0
         return carry
 
     lax.fori_loop(0, devices, clear, 0, unroll=8)
+    copies[0].wait()
+
+    def rank(b, carry):
+        owner = owner_ref[b]
+        seen = count_ref[owner]
+        count_ref[owner] = seen + 1
+        base_ref[b] = (owner * CAP + seen) * CHANNELS
+        return carry
+
+    lax.fori_loop(0, blocks, rank, 0, unroll=8)
+    for copy in copies[1:]:
+        copy.wait()
+    half = 0.5 * TAU * dist_ref[...]
+    for k in range(3):
+        coef_ref[k] = half * coef_ref[k]
+    for k in range(3, 5):
+        coef_ref[k] = TAU * coef_ref[k]
+    coef_ref[5] = jnp.where(mask_ref[...] > 0, cell_ref[...], 1 << 14).astype(f32)
 
     def place(b, carry):
-        owner = owner_ref[b]
-        rank = count_ref[owner]
-        count_ref[owner] = rank + 1
-        base = (owner * CAP + rank) * CHANNELS
+        base = base_ref[b]
         for c in range(CHANNELS):
             out_ref[pl.ds(base + c, 1), :] = coef_ref[c, pl.ds(b, 1), :]
         return carry
 
-    lax.fori_loop(0, blocks, place, 0, unroll=4)
+    lax.fori_loop(0, blocks, place, 0, unroll=8)
 
 
 def shift_rows(x, amount):
     return pltpu.roll(x, amount % x.shape[1], axis=1)
 
 
-def scatter_kernel(recv_ref, rhs_ref, perm_ref, r1_ref, wn_ref, up_ref, down_ref, first_ref, second_ref, a_ref, b_ref, acc_ref):
-    slots = recv_ref.shape[0] // CHANNELS
+def scatter_kernel(recv_ref, rhs_ref, perm_ref, r1_ref, wn_ref, up_ref, down_ref, first_ref, second_ref, acc_ref, list_ref):
+    rows = recv_ref.shape[0]
+    slots = rows // CHANNELS
     planes = rhs_ref.shape[1]
     hi_n = planes * 8
     lo_n = rhs_ref.shape[3]
     data = recv_ref[...]
-    row = lax.broadcasted_iota(jnp.int32, data.shape, 0)
-    is_cell = lax.rem(row, CHANNELS) == CHANNELS - 1
+    is_cell = lax.rem(lax.broadcasted_iota(jnp.int32, data.shape, 0), CHANNELS) == CHANNELS - 1
     cell = data.astype(jnp.int32)
     lead = data.astype(bf16).astype(f32)
-    first_ref[...] = jnp.where(is_cell, (cell >> 8).astype(f32), lead)
-    second_ref[...] = jnp.where(is_cell, (cell & 255).astype(f32), data - lead)
+    first_ref[0:rows] = jnp.where(is_cell, (cell >> 8).astype(f32), lead)
+    second_ref[0:rows] = jnp.where(is_cell, (cell & 255).astype(f32), data - lead)
+    first_ref[rows : rows + 8] = jnp.full((8, 128), -1.0, f32)
+    second_ref[rows : rows + 8] = jnp.zeros((8, 128), f32)
     acc_ref[...] = jnp.zeros(acc_ref.shape, f32)
+
+    def scan(i, count):
+        for j in range(8):
+            base = (i * 8 + j) * CHANNELS
+            list_ref[count] = base
+            mark = recv_ref[pl.ds(base + 5, 1), :][0, 0]
+            count = count + jnp.where(mark >= 0.0, 1, 0).astype(jnp.int32)
+        return count
+
+    count = lax.fori_loop(0, slots // 8, scan, jnp.int32(0))
+    for j in range(GROUP):
+        list_ref[count + j] = rows
     hi_iota = lax.broadcasted_iota(jnp.int32, (hi_n, 128), 0).astype(f32).astype(bf16)
     lo_iota = lax.broadcasted_iota(jnp.int32, (lo_n, 128), 0).astype(f32).astype(bf16)
     one = jnp.ones((), bf16)
@@ -78,21 +113,26 @@
         return jnp.concatenate([tile] * (n // 16), axis=0)
 
     def step(g, carry):
+        left, right = [], []
         for j in range(GROUP):
-            base = (g * GROUP + j) * CHANNELS
-            lanes = pl.ds(j * 128, 128)
+            base = list_ref[g * GROUP + j]
             hot = hi_iota == spread(first_ref, base + 5, hi_n)
+            pieces = []
             for c in range(5):
-                a_ref[pl.ds(2 * c * hi_n, hi_n), lanes] = jnp.where(hot, spread(first_ref, base + c, hi_n), zero)
-                a_ref[pl.ds((2 * c + 1) * hi_n, hi_n), lanes] = jnp.where(hot, spread(second_ref, base + c, hi_n), zero)
-            a_ref[pl.ds(10 * hi_n, hi_n), lanes] = jnp.where(hot, one, zero)
-            b_ref[:, lanes] = jnp.where(lo_iota == spread(second_ref, base + 5, lo_n), one, zero)
+                pieces.append(jnp.where(hot, spread(first_ref, base + c, hi_n), zero))
+                pieces.append(jnp.where(hot, spread(second_ref, base + c, hi_n), zero))
+            pieces.append(jnp.where(hot, one, zero))
+            left.append(jnp.concatenate(pieces, axis=0))
+            right.append(jnp.where(lo_iota == spread(second_ref, base + 5, lo_n), one, zero))
         acc_ref[...] += lax.dot_general(
-            a_ref[...], b_ref[...], (((1,), (1,)), ((), ())), preferred_element_type=f32
+            jnp.concatenate(left, axis=1),
+            jnp.concatenate(right, axis=1),
+            (((1,), (1,)), ((), ())),
+            preferred_element_type=f32,
         )
         return carry
 
-    lax.fori_loop(0, slots // GROUP, step, 0)
+    lax.fori_loop(0, (count + GROUP - 1) // GROUP, step, 0)
 
     def channel(c):
         if c == 5:
@@ -109,17 +149,19 @@
     for k in range(4):
         wn_ref[k] = wn[k]
     perm = perm_ref[...]
+    place = lax.axis_index("gx")
+    last = lax.axis_size("gx") - 1
     sub = lax.broadcasted_iota(jnp.int32, (planes, 8, lo_n), 1)
     t = jnp.where(sub < 3, re, shift_rows(im, 3))
     t = jnp.where(sub < 6, t, jnp.where(sub == 6, shift_rows(wn[0], 6), shift_rows(wn[1], 7)))
     up_ref[:, 0:8, :] = t
     t = jnp.where(sub < 3, perm, jnp.where(sub == 3, shift_rows(wn[2], 3), shift_rows(wn[3], 4)))
-    up_ref[:, 8:16, :] = t
+    up_ref[:, 8:16, :] = jnp.where(place == 0, 0.0, t)
     t = jnp.where(sub >= 5, re, shift_rows(im, -3))
     t = jnp.where(sub >= 2, t, jnp.where(sub == 1, shift_rows(wn[0], -6), shift_rows(wn[1], -7)))
     down_ref[:, 0:8, :] = t
     t = jnp.where(sub >= 5, perm, jnp.where(sub == 4, shift_rows(wn[2], -3), shift_rows(wn[3], -4)))
-    down_ref[:, 8:16, :] = t
+    down_ref[:, 8:16, :] = jnp.where(place == last, 0.0, t)
 
 
 ROW_PLACE = ((0, 0, 3), (0, 3, 3), (1, 0, 3), (0, 6, 1), (0, 7, 1), (1, 3, 1), (1, 4, 1))
@@ -147,7 +189,9 @@
     lo_n = perm_ref.shape[2]
     planes = perm_ref.shape[0]
     lane = lax.broadcasted_iota(jnp.int32, (planes, 16, 128), 2)
-    for out_ref, start, sign in ((left_ref, 0, 1), (right_ref, lo_n - 128, -1)):
+    position = lax.axis_index("gy")
+    last = lax.axis_size("gy") - 1
+    for out_ref, start, sign, edge in ((left_ref, 0, 1, 0), (right_ref, lo_n - 128, -1, last)):
         lanes = pl.ds(start, 128)
         place = lane if sign > 0 else 127 - lane
         strip = jnp.zeros((planes, 16, 128), f32)
@@ -158,7 +202,7 @@
             offset, width = COL_PLACE[c]
             moved = pltpu.roll(full, (sign * offset) % 128, axis=2)
             strip = jnp.where((place >= offset) & (place < offset + width), moved, strip)
-        out_ref[...] = strip
+        out_ref[...] = jnp.where(position == edge, 0.0, strip)
 
 
 def final_kernel(r1_ref, perm_ref, wn_ref, above_ref, below_ref, fleft_ref, fright_ref, sol_ref, res_ref):
@@ -247,9 +291,18 @@
     send = pl.pallas_call(
         pack_kernel,
         out_shape=shape(slots * CHANNELS, points),
-        in_specs=[pl.BlockSpec(memory_space=pltpu.SMEM)] + in_vmem(5),
+        in_specs=[pl.BlockSpec(memory_space=pl.ANY)] * 6,
         out_specs=pl.BlockSpec(memory_space=pltpu.VMEM),
-        scratch_shapes=[pltpu.SMEM((devices,), jnp.int32), pltpu.VMEM((CHANNELS, blocks, points), f32)],
+        scratch_shapes=[
+            pltpu.SMEM((blocks,), jnp.int32),
+            pltpu.SMEM((blocks,), jnp.int32),
+            pltpu.SMEM((devices,), jnp.int32),
+            pltpu.VMEM((blocks, points), f32),
+            pltpu.VMEM((CHANNELS, blocks, points), f32),
+            pltpu.VMEM((blocks, points), jnp.int32),
+            pltpu.VMEM((blocks, points), jnp.int32),
+            pltpu.SemaphoreType.DMA((6,)),
+        ],
         compiler_params=params,
         name="pack",
     )(surf_owner[:, 0], surf_dist, surf_normal, surf_inc, surf_cell, surf_mask)
@@ -262,16 +315,15 @@
         in_specs=in_vmem(3),
         out_specs=tuple(in_vmem(4)),
         scratch_shapes=[
-            pltpu.VMEM((slots * CHANNELS, points), f32),
-            pltpu.VMEM((slots * CHANNELS, points), f32),
-            pltpu.VMEM((PARTS * planes * rows, GROUP * points), bf16),
-            pltpu.VMEM((cols, GROUP * points), bf16),
+            pltpu.VMEM((slots * CHANNELS + 8, points), f32),
+            pltpu.VMEM((slots * CHANNELS + 8, points), f32),
             pltpu.VMEM((PARTS * planes * rows, cols), f32),
+            pltpu.SMEM((slots + GROUP,), jnp.int32),
         ],
         compiler_params=params,
         name="scatter",
     )(recv, rhs_field, permittivity)
-    later = [(i, i + 1) for i in range(gx - 1)]
+    later = [(i, (i + 1) % gx) for i in range(gx)]
     above = lax.ppermute(down, "gx", later)
     below = lax.ppermute(up, "gx", [(j, i) for i, j in later])
     strip = shape(planes, 16, 128)
@@ -283,7 +335,7 @@
         compiler_params=params,
         name="strips",
     )(r1, permittivity, wn, above, below)
-    later = [(i, i + 1) for i in range(gy - 1)]
+    later = [(i, (i + 1) % gy) for i in range(gy)]
     from_left = lax.ppermute(to_right, "gy", later)
     from_right = lax.ppermute(to_left, "gy", [(j, i) for i, j in later])
     return pl.pallas_call(

time: 79.2 us -> 67.5 us (0.85); the launches traced: 78.8 us -> 68.8 us
  Pallas kernels: 24.4 us -> 13 us
  starting transfers between devices: 8.33 us -> 16.5 us
  waiting for transfers between devices: 13 us -> 6.04 us
    pallas_call x1, Pallas kernels: 20.7 us -> 9.06 us  [per_device(): pl.pallas_call(scatter_kernel, out_shape=(field, shape(4, planes, rows, c...]
    ppermute x1, waiting for transfers between devices: 9.17 us -> 0.01 us  [per_device(): below = lax.ppermute(up, 'gx', [(j, i) for i, j in later])]
    ppermute x1, starting transfers between devices: 1.92 us -> 9.27 us  [per_device(): from_left = lax.ppermute(to_right, 'gy', later)]
    ppermute x1, starting transfers between devices: 1.29 us -> 6.4 us  [per_device(): below = lax.ppermute(up, 'gx', [(j, i) for i, j in later])]
    ppermute x1, starting transfers between devices: 2.41 us -> 0.01 us  [per_device(): from_right = lax.ppermute(to_left, 'gy', [(j, i) for i, j in later])]
    ppermute x1, starting transfers between devices: 2.71 us -> 0.86 us  [per_device(): above = lax.ppermute(down, 'gx', later)]
    ppermute x1, waiting for transfers between devices: 0.62 us -> 2.35 us  [per_device(): above = lax.ppermute(down, 'gx', later)]
    ppermute x1, waiting for transfers between devices: 0.01 us -> 1.33 us  [per_device(): from_left = lax.ppermute(to_right, 'gy', later)]
where the time goes in v2:
time: 67.5 us; the launch traced here: 68.8 us
  blocking collectives  27.4 us (41%)
  starting transfers between devices  16.5 us (24%)
  Pallas kernels  13 us (19%)
  waiting for transfers between devices  6.04 us (9%)
  local copies, waits for them, and re-layouts  5.01 us (7%)
  between operations  0.69 us (1%)
    all_to_all x1, blocking collectives, per_device(): lax.all_to_all(send.reshape(-1), ('gx', 'gy'), split_axis=0, concat_axis=...  27.4 us
    ppermute x1, starting transfers between devices, per_device(): from_left = lax.ppermute(to_right, 'gy', later)  9.27 us
    pallas_call x1, Pallas kernels, per_device(): pl.pallas_call(scatter_kernel, out_shape=(field, shape(4, planes, rows, c...  9.06 us
    ppermute x1, starting transfers between devices, per_device(): below = lax.ppermute(up, 'gx', [(j, i) for i, j in later])  6.4 us
    unnamed x16, local copies, waits for them, and re-layouts  5.01 us
    ppermute x1, waiting for transfers between devices, per_device(): from_right = lax.ppermute(to_left, 'gy', [(j, i) for i, j in later])  2.36 us
    ppermute x1, waiting for transfers between devices, per_device(): above = lax.ppermute(down, 'gx', later)  2.35 us
    pallas_call x1, Pallas kernels, per_device(): pl.pallas_call(pack_kernel, out_shape=shape(slots * CHANNELS, points), in...  1.89 us
  transfers between devices with their start and end apart: 4, of which 3 were waited for; matrix products, arithmetic and copies ran while one was open for 0% of the time, Pallas kernels for 0%

profile of v2, /device:TPU:1, one launch (start us, length us, event | category | flops | bytes accessed | tf_op | source)
XLA Modules:
  0.0 68.8 jit_solution(8490572380721588106)
XLA Ops:
  0.6 0.0 copy-start.7
  0.6 0.6 copy-done.7
  1.3 0.0 copy-start.1
  1.3 0.9 %copy-done.1 = f32[3,128,128]{2,1,0:T(8,128)S(1)} copy-done((f32[3,128,128]{2,1,0:T(8,128)S(1)}, f32[3,128,128]{2,1,0:T(8,128)}, u32[]{:S(2)}) %copy-start.1) | copy-done | bytes 196632
  2.2 0.0 copy-start.2
  2.2 0.9 %copy-done.2 = f32[2,128,128]{2,1,0:T(8,128)S(1)} copy-done((f32[2,128,128]{2,1,0:T(8,128)S(1)}, f32[2,128,128]{2,1,0:T(8,128)}, u32[]{:S(2)}) %copy-start.2) | copy-done | bytes 131096
  3.1 0.0 copy-start.4
  3.1 0.8 %copy-done.4 = f32[128,128]{1,0:T(8,128)S(1)} copy-done((f32[128,128]{1,0:T(8,128)S(1)}, f32[128,128]{1,0:T(8,128)}, u32[]{:S(2)}) %copy-start.4) | copy-done | bytes 65560
  4.0 0.0 copy-start.5
  4.0 0.8 %copy-done.5 = s32[128,128]{1,0:T(8,128)S(1)} copy-done((s32[128,128]{1,0:T(8,128)S(1)}, s32[128,128]{1,0:T(8,128)}, u32[]{:S(2)}) %copy-start.5) | copy-done | bytes 65560
  4.8 0.0 copy-start.6
  4.8 0.8 %copy-done.6 = s32[128,128]{1,0:T(8,128)S(1)} copy-done((s32[128,128]{1,0:T(8,128)S(1)}, s32[128,128]{1,0:T(8,128)}, u32[]{:S(2)}) %copy-start.6) | copy-done | bytes 65560
  5.6 1.9 %pack.1 = f32[1536,128]{1,0:T(8,128)S(1)} custom-call(s32[128]{0:T(128)S(1)} %bitcast.5, f32[128,128]{1,0:T(8,128)S(1)} %copy-done.4, f32[3,128,128]{2,1,0:T(8,128)S(1)} %copy-done.1, f32[2,128,128]{2,1,0:T(8,128)S(1)} %copy-done.2, s32[128,128]{1,0:T(8,128)S(1)} %copy-done.5, s32[128,128]{1,0:T(8,128)S(1)} %copy-done.6), custom_call_target="tpu_custom_call" | custom-call | tf_op jit(solution)/shard_map/pack/pallas_call | solution.py:291
  7.5 0.0 copy-start
  7.6 0.0 copy-start.3
  7.6 27.4 %all_to_all.9 = f32[128,1536,1]{1,2,0:T(1,128)S(1)} all-to-all(f32[128,1536,1]{1,2,0:T(1,128)S(1)} %bitcast.3), channel_id=1, replica_groups=mesh['gx'=32,'gy'=4] {'gx','gy'}, dimensions={0} | all-to-all | bytes 1572864 | tf_op jit(solution)/shard_map/all_to_all | solution.py:309
  35.0 0.0 copy-done
  35.0 0.0 copy-done.3
  35.0 9.1 %scatter.1 = (f32[2,8,8,256]{3,2,1,0:T(8,128)S(1)}, f32[4,8,8,256]{3,2,1,0:T(8,128)S(1)}, f32[8,16,256]{2,1,0:T(8,128)S(1)}, f32[8,16,256]{2,1,0:T(8,128)S(1)}) custom-call(f32[1536,128]{1,0:T(8,128)S(1)} %bitcast.4, f32[2,8,8,256]{3,2,1,0:T(8,128)S(1)} %copy-done.3, f32[8,8,256]{2,1,0:T(8,128)S(1)} %copy-done), custom_call_target="tpu_custom_call" | custom-call | tf_op jit(solution)/shard_map/scatter/pallas_call | solution.py:312
  44.1 0.9 %collective-permute-start = (f32[8,16,256]{2,1,0:T(8,128)S(1)}, f32[8,16,256]{2,1,0:T(8,128)S(1)}, u32[]{:S(2)}, u32[]{:S(2)}) collective-permute-start(f32[8,16,256]{2,1,0:T(8,128)S(1)} %get-tuple-element.10), channel_id=1, source_target_pairs={{0,4},{4,8},{8,12},{12,16},{16,20},{20,24},{24,28},{28,32},{32,36}... | collective-permute-start | bytes 393224 | tf_op jit(solution)/shard_map/ppermute | solution.py:327
  45.0 6.4 %collective-permute-start.1 = (f32[8,16,256]{2,1,0:T(8,128)S(1)}, f32[8,16,256]{2,1,0:T(8,128)S(1)}, u32[]{:S(2)}, u32[]{:S(2)}) collective-permute-start(f32[8,16,256]{2,1,0:T(8,128)S(1)} %get-tuple-element.11), channel_id=1, source_target_pairs={{4,0},{8,4},{12,8},{16,12},{20,16},{24,20},{28,24},{32,28},{36,32}... | collective-permute-start | bytes 393224 | tf_op jit(solution)/shard_map/ppermute | solution.py:328
  51.3 2.4 %collective-permute-done.above_ref = f32[8,16,256]{2,1,0:T(8,128)S(1)} collective-permute-done((f32[8,16,256]{2,1,0:T(8,128)S(1)}, f32[8,16,256]{2,1,0:T(8,128)S(1)}, u32[]{:S(2)}, u32[]{:S(2)}) %collective-permute-start) | collective-permute-done | bytes 131104 | tf_op jit(solution)/shard_map/ppermute | solution.py:327
  53.7 0.0 collective-permute-done.1.below_ref
  53.7 0.3 strips.1
  54.0 9.3 %collective-permute-start.2 = (f32[8,16,128]{2,1,0:T(8,128)S(1)}, f32[8,16,128]{2,1,0:T(8,128)S(1)}, u32[]{:S(2)}, u32[]{:S(2)}) collective-permute-start(f32[8,16,128]{2,1,0:T(8,128)S(1)} %get-tuple-element.12), channel_id=1, source_target_pairs={{0,1},{1,2},{2,3},{3,0},{4,5},{5,6},{6,7},{7,4},{8,9},{9,10},{10,1... | collective-permute-start | bytes 196616 | tf_op jit(solution)/shard_map/ppermute | solution.py:339
  63.2 0.0 collective-permute-start.3
  63.3 1.3 %collective-permute-done.2.fleft_ref = f32[8,16,128]{2,1,0:T(8,128)S(1)} collective-permute-done((f32[8,16,128]{2,1,0:T(8,128)S(1)}, f32[8,16,128]{2,1,0:T(8,128)S(1)}, u32[]{:S(2)}, u32[]{:S(2)}) %collective-permute-start.2) | collective-permute-done | bytes 65568 | tf_op jit(solution)/shard_map/ppermute | solution.py:339
  64.6 2.4 %collective-permute-done.3.fright_ref = f32[8,16,128]{2,1,0:T(8,128)S(1)} collective-permute-done((f32[8,16,128]{2,1,0:T(8,128)S(1)}, f32[8,16,128]{2,1,0:T(8,128)S(1)}, u32[]{:S(2)}, u32[]{:S(2)}) %collective-permute-start.3) | collective-permute-done | bytes 65568 | tf_op jit(solution)/shard_map/ppermute | solution.py:340
  66.9 1.8 %final.1 = (f32[2,8,8,256]{3,2,1,0:T(8,128)}, f32[2,8,8,256]{3,2,1,0:T(8,128)}) custom-call(f32[2,8,8,256]{3,2,1,0:T(8,128)S(1)} %get-tuple-element.8.r1_ref, f32[8,8,256]{2,1,0:T(8,128)S(1)} %copy-done, f32[4,8,8,256]{3,2,1,0:T(8,128)S(1)} %get-tuple-element.9.wn_ref, f32[8,16,256]{2,1,0:T(8,128)S(1)} %collective-permute-done.above_ref, ...), custom_call_target="tpu_custom_call" | custom-call | tf_op jit(solution)/shard_map/final/pallas_call | solution.py:341
Async XLA Ops:
  0.6 0.7 copy-start.7
  1.3 0.9 %copy-start.1 = (f32[3,128,128]{2,1,0:T(8,128)S(1)}, f32[3,128,128]{2,1,0:T(8,128)}, u32[]{:S(2)}) copy-start(f32[3,128,128]{2,1,0:T(8,128)} %normal_hbm.1) | copy-start | bytes 589828
  2.2 0.9 %copy-start.2 = (f32[2,128,128]{2,1,0:T(8,128)S(1)}, f32[2,128,128]{2,1,0:T(8,128)}, u32[]{:S(2)}) copy-start(f32[2,128,128]{2,1,0:T(8,128)} %inc_hbm.1) | copy-start | bytes 393220
  3.1 0.8 %copy-start.4 = (f32[128,128]{1,0:T(8,128)S(1)}, f32[128,128]{1,0:T(8,128)}, u32[]{:S(2)}) copy-start(f32[128,128]{1,0:T(8,128)} %dist_hbm.1) | copy-start | bytes 196612
  4.0 0.8 %copy-start.5 = (s32[128,128]{1,0:T(8,128)S(1)}, s32[128,128]{1,0:T(8,128)}, u32[]{:S(2)}) copy-start(s32[128,128]{1,0:T(8,128)} %cell_hbm.1) | copy-start | bytes 196612
  4.8 0.8 %copy-start.6 = (s32[128,128]{1,0:T(8,128)S(1)}, s32[128,128]{1,0:T(8,128)}, u32[]{:S(2)}) copy-start(s32[128,128]{1,0:T(8,128)} %mask_hbm.1) | copy-start | bytes 196612
  7.5 27.5 %copy-start = (f32[8,8,256]{2,1,0:T(8,128)S(1)}, f32[8,8,256]{2,1,0:T(8,128)}, u32[]{:S(2)}) copy-start(f32[8,8,256]{2,1,0:T(8,128)} %perm_ref.5) | copy-start | bytes 196612
  7.6 27.5 %copy-start.3 = (f32[2,8,8,256]{3,2,1,0:T(8,128)S(1)}, f32[2,8,8,256]{3,2,1,0:T(8,128)}, u32[]{:S(2)}) copy-start(f32[2,8,8,256]{3,2,1,0:T(8,128)} %rhs_ref.1) | copy-start | bytes 393220
  44.1 9.6 %collective-permute-start = (f32[8,16,256]{2,1,0:T(8,128)S(1)}, f32[8,16,256]{2,1,0:T(8,128)S(1)}, u32[]{:S(2)}, u32[]{:S(2)}) collective-permute-start(f32[8,16,256]{2,1,0:T(8,128)S(1)} %get-tuple-element.10), channel_id=1, source_target_pairs={{0,4},{4,8},{8,12},{12,16},{16,20},{20,24},{24,28},{28,32},{32,36}... | collective-permute-start | bytes 393224 | tf_op jit(solution)/shard_map/ppermute | solution.py:327
  45.0 8.8 %collective-permute-start.1 = (f32[8,16,256]{2,1,0:T(8,128)S(1)}, f32[8,16,256]{2,1,0:T(8,128)S(1)}, u32[]{:S(2)}, u32[]{:S(2)}) collective-permute-start(f32[8,16,256]{2,1,0:T(8,128)S(1)} %get-tuple-element.11), channel_id=1, source_target_pairs={{4,0},{8,4},{12,8},{16,12},{20,16},{24,20},{28,24},{32,28},{36,32}... | collective-permute-start | bytes 393224 | tf_op jit(solution)/shard_map/ppermute | solution.py:328
  54.0 10.6 %collective-permute-start.2 = (f32[8,16,128]{2,1,0:T(8,128)S(1)}, f32[8,16,128]{2,1,0:T(8,128)S(1)}, u32[]{:S(2)}, u32[]{:S(2)}) collective-permute-start(f32[8,16,128]{2,1,0:T(8,128)S(1)} %get-tuple-element.12), channel_id=1, source_target_pairs={{0,1},{1,2},{2,3},{3,0},{4,5},{5,6},{6,7},{7,4},{8,9},{9,10},{10,1... | collective-permute-start | bytes 196616 | tf_op jit(solution)/shard_map/ppermute | solution.py:339
  63.2 3.7 %collective-permute-start.3 = (f32[8,16,128]{2,1,0:T(8,128)S(1)}, f32[8,16,128]{2,1,0:T(8,128)S(1)}, u32[]{:S(2)}, u32[]{:S(2)}) collective-permute-start(f32[8,16,128]{2,1,0:T(8,128)S(1)} %get-tuple-element.13), channel_id=1, source_target_pairs={{1,0},{2,1},{3,2},{0,3},{5,4},{6,5},{7,6},{4,7},{9,8},{10,9},{11,1... | collective-permute-start | bytes 196616 | tf_op jit(solution)/shard_map/ppermute | solution.py:340
